TPU v7x, 32 devices: a whole 2x2x4 slice. The times are simulated.
32 devices in a mesh: row: 4 (over y, core), col: 8 (over z, x).
Axes of the slice: x: 2, y: 2, z: 4, core: 2. Of those that a mesh axis runs over, the one named last changes fastest.
Arguments:
- measured: float32 [1024, 3072], P('row', 'col'), may hold values from -32 to 32
- denoised: float32 [1024, 3072], P('row', 'col'), may hold values from -6 to 6
- reg_weight: float32 [1], replicated, may hold values from 0.5 to 2
- left_blocks: bfloat16 [2, 8, 3, 128, 128], replicated, may hold values from -0.3125 to 0.3125
- left_cols: int32 [2, 8, 3], replicated, may hold values from 0 to 7, as said below
- right_blocks: bfloat16 [2, 24, 3, 128, 128], replicated, may hold values from -0.3125 to 0.3125
- right_cols: int32 [2, 24, 3], replicated, may hold values from 0 to 23, as said below
Outputs:
- solution: float32 [1024, 3072], P('row', 'col')
- residual: float32 [1024, 3072], P('row', 'col')
Inputs may be any that keep to these rules, and one draw needn't show every extreme that they name: `left_cols`: the three block columns of each block row of A_k are distinct and lie within 2 of that row's own block index. `right_cols`: the three block columns of each block row of B_k are distinct and lie within 2 of that row's own block index.
All inputs are finite; a program needn't handle non-finite values.
Results may differ from a plain program's by a relative error of at most 0.017.
Values may be sent and summed in bfloat16 or wider, within the bound.
A program may use at most 128 MiB of HBM per device.

v0:
```python
import jax
import jax.numpy as jnp
from jax import lax
from jax.sharding import PartitionSpec as P

ITERS = 2


def padded(block, sides, width):
    for axis, dim in sides:
        count = lax.axis_size(axis)
        forward = [(i, i + 1) for i in range(count - 1)]
        backward = [(target, source) for source, target in forward]
        low = lax.ppermute(
            lax.slice_in_dim(block, block.shape[dim] - width, None, axis=dim), axis, forward
        )
        high = lax.ppermute(lax.slice_in_dim(block, 0, width, axis=dim), axis, backward)
        block = jnp.concatenate([low, block, high], axis=dim)
    return block


def band_window(blocks, block_cols, first, block_count):
    total = blocks.shape[1]
    row_ids = first - 2 + jnp.arange(block_count + 4, dtype=jnp.int32)
    inside = (row_ids >= 0) & (row_ids < total)
    clipped = jnp.clip(row_ids, 0, total - 1)
    window = jnp.take(blocks, clipped, axis=1)
    relative = jnp.take(block_cols, clipped, axis=1) - (first - 2)
    relative = jnp.where(inside[None, :, None], relative, -100)
    return (window, relative)


def rows_forward(window, relative, margined):
    block_count = margined.shape[0] - 4
    picked = margined[relative[2 : block_count + 2]]
    return jnp.einsum(
        "ijab,ijbw->iaw", window[2 : block_count + 2], picked, preferred_element_type=jnp.float32
    )


def rows_adjoint(window, relative, margined):
    block_count = margined.shape[0] - 4
    terms = jnp.einsum("tjab,taw->tjbw", window, margined, preferred_element_type=jnp.float32)
    targets = (jnp.arange(block_count, dtype=jnp.int32) + 2)[:, None]
    running = jnp.zeros((block_count,) + terms.shape[2:], jnp.float32)
    for shift_index in range(5):
        selected = (relative[shift_index : shift_index + block_count] == targets).astype(
            jnp.float32
        )
        running = running + jnp.sum(
            selected[:, :, None, None] * terms[shift_index : shift_index + block_count], axis=1
        )
    return running


def cols_forward(window, relative, margined):
    block_count = margined.shape[1] - 4
    picked = margined[:, relative[2 : block_count + 2]]
    return jnp.einsum(
        "rcjb,cjab->rca", picked, window[2 : block_count + 2], preferred_element_type=jnp.float32
    )


def cols_adjoint(window, relative, margined):
    block_count = margined.shape[1] - 4
    terms = jnp.einsum("rta,tjab->rtjb", margined, window, preferred_element_type=jnp.float32)
    targets = (jnp.arange(block_count, dtype=jnp.int32) + 2)[:, None]
    running = jnp.zeros((terms.shape[0], block_count, terms.shape[3]), jnp.float32)
    for shift_index in range(5):
        selected = (relative[shift_index : shift_index + block_count] == targets).astype(
            jnp.float32
        )
        running = running + jnp.sum(
            selected[None, :, :, None] * terms[:, shift_index : shift_index + block_count], axis=2
        )
    return running


def row_margin(stacked, block_size):
    widened = padded(stacked, (("row", 1),), 2 * block_size)
    return widened.reshape(widened.shape[0], -1, block_size, widened.shape[2])


def column_section(stacked, window, relative, paired, block_size):
    regrouped = lax.all_to_all(stacked, "col", split_axis=1, concat_axis=2, tiled=True)
    margined = regrouped.reshape(regrouped.shape[0], regrouped.shape[1], -1, block_size)
    margined = jnp.pad(margined, ((0, 0), (0, 0), (2, 2), (0, 0)))
    if paired:
        result = (
            cols_adjoint(window[0], relative[0], margined[0])
            + cols_adjoint(window[1], relative[1], margined[1])
        )[None]
    else:
        result = jnp.stack(
            [
                cols_forward(window[0], relative[0], margined[0]),
                cols_forward(window[1], relative[1], margined[0]),
            ]
        )
    result = result.astype(jnp.bfloat16)
    result = result.reshape(result.shape[0], result.shape[1], -1)
    result = lax.all_to_all(result, "col", split_axis=2, concat_axis=1, tiled=True)
    return result


def global_squares(values):
    return lax.psum(jnp.sum(values * values), ("row", "col"))


def shards(measured, denoised, reg_weight, left_blocks, left_cols, right_blocks, right_cols):
    block_size = left_blocks.shape[-1]
    height, breadth = measured.shape
    row_count = height // block_size
    left_window, left_relative = band_window(
        left_blocks, left_cols, lax.axis_index("row") * row_count, row_count
    )
    right_window, right_relative = band_window(right_blocks, right_cols, 0, right_blocks.shape[1])
    weight = reg_weight[0]

    def forward(source):
        rounded = source.astype(jnp.bfloat16)
        inner = column_section(rounded[None], right_window, right_relative, False, block_size)
        margined = row_margin(inner, block_size)
        running = rows_forward(left_window[0], left_relative[0], margined[0]) + rows_forward(
            left_window[1], left_relative[1], margined[1]
        )
        return running.reshape(height, breadth)

    def adjoint(source):
        rounded = source.astype(jnp.bfloat16)
        margined = row_margin(rounded[None], block_size)
        inner = jnp.stack(
            [
                rows_adjoint(left_window[factor], left_relative[factor], margined[0])
                for factor in range(2)
            ]
        ).astype(jnp.bfloat16)
        inner = inner.reshape(2, height, breadth)
        summed = column_section(inner, right_window, right_relative, True, block_size)[0]
        return lax.optimization_barrier(summed).astype(jnp.float32)

    rhs_field = adjoint(measured) + weight * denoised
    solution = jnp.zeros((height, breadth), jnp.float32)
    residual = rhs_field
    direction = rhs_field
    norm_now = global_squares(residual)
    for iteration in range(ITERS):
        applied = adjoint(forward(direction)) + weight * direction
        step_size = norm_now / lax.psum(jnp.sum(direction * applied), ("row", "col"))
        solution = solution + step_size * direction
        residual = residual - step_size * applied
        if iteration + 1 < ITERS:
            norm_next = global_squares(residual)
            direction = residual + norm_next / (norm_now + 1e-06) * direction
            norm_now = norm_next
    return (solution, residual)


def solution(mesh):
    return jax.shard_map(
        shards,
        mesh=mesh,
        in_specs=(P("row", "col"), P("row", "col"), P(), P(), P(), P(), P()),
        out_specs=(P("row", "col"), P("row", "col")),
        check_vma=False,
    )
```

profile of v0, /device:TPU:0, one launch (start us, length us, event | category | flops | bytes accessed | tf_op | source)
XLA Modules:
  0.0 465.3 jit_solution(11481940712808641357)
XLA Ops:
  3.1 3.0 collective-permute-start
  17.8 7.4 %all-to-all-start = ((bf16[2,256,384]{2,0,1:T(2,128)(2,1)}), bf16[2,256,384]{2,0,1:T(2,128)(2,1)S(1)}, u32[]{:S(2)}, u32[]{:S(2)}) async-start(bf16[2,256,384]{2,0,1:T(2,128)(2,1)} %copy.198), calls=%async_computation | async-start | bytes 786432 | tf_op jit(solution)/shard_map/all_to_all | solution.py:85
  26.2 6.1 %gather_fusion.1 = bf16[28,2,3,128,128]{4,3,2,1,0:T(8,128)(2,1)} fusion(bf16[2,24,3,128,128]{4,3,2,1,0:T(8,128)(2,1)} %param.12, s32[1024]{0:T(1024)S(1)} %pad_clamp_fusion.5), kind=kCustom, calls=%fused_computation.1 | custom fusion | bytes 11010160 | tf_op jit(solution)/shard_map/jit(_take)/gather | solution.py:27
  32.3 5.6 %fusion = bf16[2,28,3,128,128]{4,3,2,1,0:T(8,128)(2,1)} fusion(bf16[28,2,3,128,128]{4,3,2,1,0:T(8,128)(2,1)} %gather_fusion.1, pred[28]{0:T(512)(128)(4,1)S(1)} %get-tuple-element.114), kind=kLoop, calls=%fused_computation.13 | loop fusion | flops 2752512 | bytes 11010076 | tf_op jit(solution)/shard_map/jit(_take)/select_n | solution.py:27
  38.7 2.4 fusion.13
  41.1 2.4 fusion.16
  46.5 1.8 copy.221
  48.9 17.9 %reduce = bf16[3072,32]{1,0:T(8,128)(2,1)} reduce(bf16[3072,1,32]{2,1,0:T(2,128)(2,1)S(1)} %bitcast.411, bf16[]{:T(256)} %broadcast.612), dimensions={1}, to_apply=%bitcast.365.reduce_sub_computation | reduce | bytes 393218
  66.8 2.5 reshape.1504
  69.3 5.9 %all-to-all-start.1 = ((bf16[8,2,6144]{2,1,0:T(2,128)(2,1)}), bf16[8,2,6144]{2,1,0:T(2,128)(2,1)S(1)}, u32[]{:S(2)}, u32[]{:S(2)}) async-start(bf16[8,2,6144]{2,1,0:T(2,128)(2,1)} %reshape.1504), calls=%async_computation.1 | async-start | bytes 393216 | tf_op jit(solution)/shard_map/all_to_all | solution.py:102
  76.7 7.2 %all-to-all-done.1 = bf16[8,2,6144]{2,1,0:T(2,128)(2,1)S(1)} async-done(((bf16[8,2,6144]{2,1,0:T(2,128)(2,1)}), bf16[8,2,6144]{2,1,0:T(2,128)(2,1)S(1)}, u32[]{:S(2)}, u32[]{:S(2)}) %all-to-all-start.1) | async-done | bytes 196640 | tf_op jit(solution)/shard_map/all_to_all | solution.py:102
  89.1 3.4 all-to-all-start.2
  92.7 7.6 %all-to-all-done.2 = bf16[8,2,6144]{2,1,0:T(2,128)(2,1)S(1)} async-done(((bf16[8,2,6144]{2,1,0:T(2,128)(2,1)}), bf16[8,2,6144]{2,1,0:T(2,128)(2,1)S(1)}, u32[]{:S(2)}, u32[]{:S(2)}) %all-to-all-start.2) | async-done | bytes 196640 | tf_op jit(solution)/shard_map/all_to_all | solution.py:85
  101.4 2.6 fusion.89
  104.9 2.6 fusion.91
  107.7 1.9 copy.233
  109.6 2.2 reshape.1508
  111.8 3.5 all-to-all-start.3
  116.4 9.9 %all-to-all-done.3 = bf16[8,2,12288]{2,1,0:T(2,128)(2,1)S(1)} async-done(((bf16[8,2,12288]{2,1,0:T(2,128)(2,1)}), bf16[8,2,12288]{2,1,0:T(2,128)(2,1)S(1)}, u32[]{:S(2)}, u32[]{:S(2)}) %all-to-all-start.3) | async-done | bytes 393248 | tf_op jit(solution)/shard_map/all_to_all | solution.py:102
  129.5 3.1 collective-permute-start.2
  139.5 5.9 %collective-permute-start.4 = (bf16[1,256,384]{2,1,0:T(8,128)(2,1)S(1)}, bf16[1,256,384]{2,1,0:T(8,128)(2,1)S(1)}, u32[]{:S(2)}, u32[]{:S(2)}) collective-permute-start(bf16[1,256,384]{2,1,0:T(8,128)(2,1)S(1)} %bitcast.469), channel_id=1, source_target_pairs={{0,8},{8,16},{16,24},{1,9},{9,17},{17,25},{2,10},{10,18},{18,26},{... | collective-permute-start | bytes 589832 | tf_op jit(solution)/shard_map/ppermute | solution.py:14
  149.7 14.0 %all_to_all.156 = bf16[2,256,384]{2,0,1:T(2,128)(2,1)S(1)} all-to-all(bf16[2,256,384]{2,0,1:T(2,128)(2,1)S(1)} %copy.238), channel_id=1, replica_groups=mesh['row'=4,'col'=8] {'col'}, dimensions={1} | all-to-all | bytes 786432 | tf_op jit(solution)/shard_map/all_to_all | solution.py:85
  164.1 2.4 fusion.12
  166.6 2.4 fusion.15
  172.1 1.8 copy.243
  173.9 17.9 %reduce.2 = bf16[3072,32]{1,0:T(8,128)(2,1)} reduce(bf16[3072,1,32]{2,1,0:T(2,128)(2,1)S(1)} %bitcast.414, bf16[]{:T(256)} %broadcast.612), dimensions={1}, to_apply=%bitcast.371.reduce_sub_computation | reduce | bytes 393218
  191.8 1.9 reshape.1510
  193.6 14.9 %all_to_all.157 = bf16[8,2,6144]{2,1,0:T(2,128)(2,1)S(1)} all-to-all(bf16[8,2,6144]{2,1,0:T(2,128)(2,1)S(1)} %reshape.1510), channel_id=1, replica_groups=mesh['row'=4,'col'=8] {'col'}, dimensions={0} | all-to-all | bytes 393216 | tf_op jit(solution)/shard_map/all_to_all | solution.py:102
  211.6 39.3 %all-reduce.5 = (f32[]{:T(128)}, f32[]{:T(128)}) all-reduce(f32[]{:T(128)} %get-tuple-element.63, f32[]{:T(128)} %get-tuple-element.62), channel_id=1, replica_groups=mesh['row'=4,'col'=8] {'row','col'}, use_global_device_ids=true, to_apply=%region_21.22 | all-reduce | flops 2 | bytes 16 | tf_op jit(solution)/shard_map/psum | solution.py:107
  253.5 41.3 %psum.30 = f32[]{:T(128)} all-reduce(f32[]{:T(128)} %multiply_reduce_fusion.1), channel_id=1, replica_groups=mesh['row'=4,'col'=8] {'row','col'}, use_global_device_ids=true, to_apply=%region_45.46 | all-reduce | flops 1 | bytes 8 | tf_op jit(solution)/shard_map/psum | solution.py:107
  297.8 12.1 %all_to_all.158 = bf16[8,2,6144]{2,1,0:T(2,128)(2,1)S(1)} all-to-all(bf16[8,2,6144]{2,1,0:T(2,128)(2,1)S(1)} %reshape.1512), channel_id=1, replica_groups=mesh['row'=4,'col'=8] {'col'}, dimensions={0} | all-to-all | bytes 393216 | tf_op jit(solution)/shard_map/all_to_all | solution.py:85
  311.7 2.6 fusion.90
  314.5 2.6 fusion.92
  317.3 3.0 copy.251
  320.3 4.2 reshape.1514
  324.5 11.9 %all_to_all.159 = bf16[8,2,12288]{2,1,0:T(2,128)(2,1)S(1)} all-to-all(bf16[8,2,12288]{2,1,0:T(2,128)(2,1)S(1)} %reshape.1514), channel_id=1, replica_groups=mesh['row'=4,'col'=8] {'col'}, dimensions={0} | all-to-all | bytes 786432 | tf_op jit(solution)/shard_map/all_to_all | solution.py:102
  336.4 1.9 reshape.1515
  338.3 3.5 copy.288
  343.2 3.1 collective-permute-start.6
  349.4 1.9 gather_fusion.11
  353.3 7.0 %collective-permute-start.8 = (bf16[1,256,384]{2,1,0:T(8,128)(2,1)S(1)}, bf16[1,256,384]{2,1,0:T(8,128)(2,1)S(1)}, u32[]{:S(2)}, u32[]{:S(2)}) collective-permute-start(bf16[1,256,384]{2,1,0:T(8,128)(2,1)S(1)} %bitcast.472), channel_id=1, source_target_pairs={{0,8},{8,16},{16,24},{1,9},{9,17},{17,25},{2,10},{10,18},{18,26},{... | collective-permute-start | bytes 589832 | tf_op jit(solution)/shard_map/ppermute | solution.py:14
  364.6 12.9 %all_to_all.160 = bf16[2,256,384]{2,0,1:T(2,128)(2,1)S(1)} all-to-all(bf16[2,256,384]{2,0,1:T(2,128)(2,1)S(1)} %copy.256), channel_id=1, replica_groups=mesh['row'=4,'col'=8] {'col'}, dimensions={1} | all-to-all | bytes 786432 | tf_op jit(solution)/shard_map/all_to_all | solution.py:85
  378.0 2.4 fusion.11
  380.4 2.4 fusion.14
  385.9 1.8 copy.261
  387.7 16.9 %reduce.4 = bf16[3072,32]{1,0:T(8,128)(2,1)S(1)} reduce(bf16[3072,1,32]{2,1,0:T(2,128)(2,1)S(1)} %bitcast.412, bf16[]{:T(256)} %broadcast.612), dimensions={1}, to_apply=%bitcast.377.reduce_sub_computation | reduce | bytes 393218
  405.4 14.9 %all_to_all.161 = bf16[8,2,6144]{2,1,0:T(2,128)(2,1)S(1)} all-to-all(bf16[8,2,6144]{2,1,0:T(2,128)(2,1)S(1)} %reshape.1516), channel_id=1, replica_groups=mesh['row'=4,'col'=8] {'col'}, dimensions={0} | all-to-all | bytes 393216 | tf_op jit(solution)/shard_map/all_to_all | solution.py:102
  423.4 39.3 %psum.31 = f32[]{:T(128)} all-reduce(f32[]{:T(128)} %multiply_reduce_fusion), channel_id=1, replica_groups=mesh['row'=4,'col'=8] {'row','col'}, use_global_device_ids=true, to_apply=%region_67.68 | all-reduce | flops 1 | bytes 8 | tf_op jit(solution)/shard_map/psum | solution.py:149
  (321 shorter events, 73.1 us)
Async XLA Ops:
  0.6 9.5 %copy-start = (bf16[2,8,3,128,128]{4,3,2,1,0:T(8,128)(2,1)S(1)}, bf16[2,8,3,128,128]{4,3,2,1,0:T(8,128)(2,1)}, u32[]{:S(2)}) copy-start(bf16[2,8,3,128,128]{4,3,2,1,0:T(8,128)(2,1)} %param.10) | copy-start | bytes 4718596
  1.8 12.1 %collective-permute-start.1 = (bf16[1,256,384]{2,1,0:T(8,128)(2,1)S(1)}, bf16[1,256,384]{2,1,0:T(8,128)(2,1)S(1)}, u32[]{:S(2)}, u32[]{:S(2)}) collective-permute-start(bf16[1,256,384]{2,1,0:T(8,128)(2,1)S(1)} %convert_bitcast_fusion.2), channel_id=1, source_target_pairs={{8,0},{16,8},{24,16},{9,1},{17,9},{25,17},{10,2},{18,10},{26,18},{... | collective-permute-start | bytes 589832 | tf_op jit(solution)/shard_map/ppermute | solution.py:17
  3.1 10.9 %collective-permute-start = (bf16[1,256,384]{2,1,0:T(8,128)(2,1)S(1)}, bf16[1,256,384]{2,1,0:T(8,128)(2,1)S(1)}, u32[]{:S(2)}, u32[]{:S(2)}) collective-permute-start(bf16[1,256,384]{2,1,0:T(8,128)(2,1)S(1)} %convert_bitcast_fusion.2), channel_id=1, source_target_pairs={{0,8},{8,16},{16,24},{1,9},{9,17},{17,25},{2,10},{10,18},{18,26},{... | collective-permute-start | bytes 589832 | tf_op jit(solution)/shard_map/ppermute | solution.py:14
  7.7 6.1 %copy-start.57 = (s32[1,2,3]{2,0,1:T(1,128)}, s32[1,2,3]{2,0,1:T(1,128)S(1)}, u32[]{:S(2)}) copy-start(s32[1,2,3]{2,0,1:T(1,128)S(1)} %get-tuple-element.87) | copy-start | bytes 76
  7.7 6.1 %copy-start.58 = (s32[1,2,3]{2,0,1:T(1,128)}, s32[1,2,3]{2,0,1:T(1,128)S(1)}, u32[]{:S(2)}) copy-start(s32[1,2,3]{2,0,1:T(1,128)S(1)} %get-tuple-element.92) | copy-start | bytes 76
  13.9 1.4 copy-start.48
  13.9 1.4 copy-start.51
  13.9 1.4 copy-start.54
  13.9 2.0 copy-start.33
  13.9 2.0 copy-start.36
  13.9 2.0 copy-start.39
  17.8 20.4 %all-to-all-start = ((bf16[2,256,384]{2,0,1:T(2,128)(2,1)}), bf16[2,256,384]{2,0,1:T(2,128)(2,1)S(1)}, u32[]{:S(2)}, u32[]{:S(2)}) async-start(bf16[2,256,384]{2,0,1:T(2,128)(2,1)} %copy.198), calls=%async_computation | async-start | bytes 786432 | tf_op jit(solution)/shard_map/all_to_all | solution.py:85
  25.4 19.2 %copy-start.9 = (f32[24,3]{1,0:T(8,128)}, f32[24,3]{1,0:T(8,128)S(1)}, u32[]{:S(2)}) copy-start(f32[24,3]{1,0:T(8,128)S(1)} %copy.194) | copy-start | bytes 868
  25.5 19.2 %copy-start.15 = (f32[24,3]{1,0:T(8,128)}, f32[24,3]{1,0:T(8,128)S(1)}, u32[]{:S(2)}) copy-start(f32[24,3]{1,0:T(8,128)S(1)} %copy.203) | copy-start | bytes 868
  25.6 19.1 %copy-start.21 = (f32[24,3]{1,0:T(8,128)}, f32[24,3]{1,0:T(8,128)S(1)}, u32[]{:S(2)}) copy-start(f32[24,3]{1,0:T(8,128)S(1)} %copy.205) | copy-start | bytes 868
  25.7 19.0 %copy-start.24 = (f32[24,3]{1,0:T(8,128)}, f32[24,3]{1,0:T(8,128)S(1)}, u32[]{:S(2)}) copy-start(f32[24,3]{1,0:T(8,128)S(1)} %copy.207) | copy-start | bytes 868
  25.8 18.9 %copy-start.30 = (f32[24,3]{1,0:T(8,128)}, f32[24,3]{1,0:T(8,128)S(1)}, u32[]{:S(2)}) copy-start(f32[24,3]{1,0:T(8,128)S(1)} %copy.209) | copy-start | bytes 868
  25.8 17.6 %copy-start.3 = (f32[24,3]{1,0:T(8,128)}, f32[24,3]{1,0:T(8,128)S(1)}, u32[]{:S(2)}) copy-start(f32[24,3]{1,0:T(8,128)S(1)} %copy.211) | copy-start | bytes 868
  25.9 17.5 %copy-start.6 = (f32[24,3]{1,0:T(8,128)}, f32[24,3]{1,0:T(8,128)S(1)}, u32[]{:S(2)}) copy-start(f32[24,3]{1,0:T(8,128)S(1)} %copy.213) | copy-start | bytes 868
  26.0 17.4 %copy-start.12 = (f32[24,3]{1,0:T(8,128)}, f32[24,3]{1,0:T(8,128)S(1)}, u32[]{:S(2)}) copy-start(f32[24,3]{1,0:T(8,128)S(1)} %copy.215) | copy-start | bytes 868
  26.1 17.4 %copy-start.18 = (f32[24,3]{1,0:T(8,128)}, f32[24,3]{1,0:T(8,128)S(1)}, u32[]{:S(2)}) copy-start(f32[24,3]{1,0:T(8,128)S(1)} %copy.217) | copy-start | bytes 868
  26.2 17.3 %copy-start.27 = (f32[24,3]{1,0:T(8,128)}, f32[24,3]{1,0:T(8,128)S(1)}, u32[]{:S(2)}) copy-start(f32[24,3]{1,0:T(8,128)S(1)} %copy.219) | copy-start | bytes 868
  69.3 14.5 %all-to-all-start.1 = ((bf16[8,2,6144]{2,1,0:T(2,128)(2,1)}), bf16[8,2,6144]{2,1,0:T(2,128)(2,1)S(1)}, u32[]{:S(2)}, u32[]{:S(2)}) async-start(bf16[8,2,6144]{2,1,0:T(2,128)(2,1)} %reshape.1504), calls=%async_computation.1 | async-start | bytes 393216 | tf_op jit(solution)/shard_map/all_to_all | solution.py:102
  84.7 1.5 copy-start.2
  86.3 6.4 %copy-start.61 = (s32[72]{0:T(128)S(1)}, s32[72]{0:T(128)}, u32[]{:S(2)}) copy-start(s32[72]{0:T(128)} %reshape.1417) | copy-start | bytes 868
  89.1 11.2 %all-to-all-start.2 = ((bf16[8,2,6144]{2,1,0:T(2,128)(2,1)}), bf16[8,2,6144]{2,1,0:T(2,128)(2,1)S(1)}, u32[]{:S(2)}, u32[]{:S(2)}) async-start(bf16[8,2,6144]{2,1,0:T(2,128)(2,1)} %reshape.1506), calls=%async_computation.2 | async-start | bytes 393216 | tf_op jit(solution)/shard_map/all_to_all | solution.py:85
  111.8 14.6 %all-to-all-start.3 = ((bf16[8,2,12288]{2,1,0:T(2,128)(2,1)}), bf16[8,2,12288]{2,1,0:T(2,128)(2,1)S(1)}, u32[]{:S(2)}, u32[]{:S(2)}) async-start(bf16[8,2,12288]{2,1,0:T(2,128)(2,1)} %reshape.1508), calls=%async_computation.3 | async-start | bytes 786432 | tf_op jit(solution)/shard_map/all_to_all | solution.py:102
  128.2 5.7 %collective-permute-start.3 = (bf16[2,256,384]{2,1,0:T(8,128)(2,1)S(1)}, bf16[2,256,384]{2,1,0:T(8,128)(2,1)S(1)}, u32[]{:S(2)}, u32[]{:S(2)}) collective-permute-start(bf16[2,256,384]{2,1,0:T(8,128)(2,1)S(1)} %bitcast.444), channel_id=1, source_target_pairs={{8,0},{16,8},{24,16},{9,1},{17,9},{25,17},{10,2},{18,10},{26,18},{... | collective-permute-start | bytes 1179656 | tf_op jit(solution)/shard_map/ppermute | solution.py:17
  129.5 4.4 collective-permute-start.2
  133.3 1.7 copy-start.59
  133.9 3.2 copy-start.60
  138.2 7.2 %collective-permute-start.5 = (bf16[1,256,384]{2,1,0:T(8,128)(2,1)S(1)}, bf16[1,256,384]{2,1,0:T(8,128)(2,1)S(1)}, u32[]{:S(2)}, u32[]{:S(2)}) collective-permute-start(bf16[1,256,384]{2,1,0:T(8,128)(2,1)S(1)} %bitcast.468), channel_id=1, source_target_pairs={{8,0},{16,8},{24,16},{9,1},{17,9},{25,17},{10,2},{18,10},{26,18},{... | collective-permute-start | bytes 589832 | tf_op jit(solution)/shard_map/ppermute | solution.py:17
  139.5 6.9 %collective-permute-start.4 = (bf16[1,256,384]{2,1,0:T(8,128)(2,1)S(1)}, bf16[1,256,384]{2,1,0:T(8,128)(2,1)S(1)}, u32[]{:S(2)}, u32[]{:S(2)}) collective-permute-start(bf16[1,256,384]{2,1,0:T(8,128)(2,1)S(1)} %bitcast.469), channel_id=1, source_target_pairs={{0,8},{8,16},{16,24},{1,9},{9,17},{17,25},{2,10},{10,18},{18,26},{... | collective-permute-start | bytes 589832 | tf_op jit(solution)/shard_map/ppermute | solution.py:14
  166.5 2.5 copy-start.4
  166.5 2.5 copy-start.7
  166.5 2.5 copy-start.13
  166.5 2.5 copy-start.19
  166.5 2.5 copy-start.28
  341.9 4.4 collective-permute-start.7
  343.2 4.4 collective-permute-start.6
  352.0 8.3 %collective-permute-start.9 = (bf16[1,256,384]{2,1,0:T(8,128)(2,1)S(1)}, bf16[1,256,384]{2,1,0:T(8,128)(2,1)S(1)}, u32[]{:S(2)}, u32[]{:S(2)}) collective-permute-start(bf16[1,256,384]{2,1,0:T(8,128)(2,1)S(1)} %bitcast.471), channel_id=1, source_target_pairs={{8,0},{16,8},{24,16},{9,1},{17,9},{25,17},{10,2},{18,10},{26,18},{... | collective-permute-start | bytes 589832 | tf_op jit(solution)/shard_map/ppermute | solution.py:17
  353.3 8.0 %collective-permute-start.8 = (bf16[1,256,384]{2,1,0:T(8,128)(2,1)S(1)}, bf16[1,256,384]{2,1,0:T(8,128)(2,1)S(1)}, u32[]{:S(2)}, u32[]{:S(2)}) collective-permute-start(bf16[1,256,384]{2,1,0:T(8,128)(2,1)S(1)} %bitcast.472), channel_id=1, source_target_pairs={{0,8},{8,16},{16,24},{1,9},{9,17},{17,25},{2,10},{10,18},{18,26},{... | collective-permute-start | bytes 589832 | tf_op jit(solution)/shard_map/ppermute | solution.py:14
  380.4 2.5 copy-start.11
  380.4 2.5 copy-start.17
  380.4 2.5 copy-start.23
  380.4 2.5 copy-start.26
  380.4 2.5 copy-start.32
  422.6 42.5 %copy-start.1 = (bf16[2,8,3,128,128]{4,3,2,1,0:T(8,128)(2,1)S(1)}, bf16[2,8,3,128,128]{4,3,2,1,0:T(8,128)(2,1)}, u32[]{:S(2)}) copy-start(bf16[2,8,3,128,128]{4,3,2,1,0:T(8,128)(2,1)} %param.10) | copy-start | bytes 4718596
  (28 other events, 25.4 us)
where the time goes:
time: 471 us; the launch traced here: 465 us
  blocking collectives  201 us (43%)
  other arithmetic  81.6 us (17%)
  local copies, waits for them, and re-layouts  69.2 us (15%)
  starting transfers between devices  48.6 us (10%)
  matrix products  29.6 us (6%)
  waiting for transfers between devices  28.4 us (6%)
  between operations  7.32 us (2%)
    psum x2, blocking collectives, global_squares(): return lax.psum(jnp.sum(values * values), ('row', 'col'))  80.7 us
    unnamed x5, other arithmetic  56.2 us
    all_to_all x3, blocking collectives, column_section(): lax.all_to_all(result, 'col', split_axis=2, concat_axis=1, tiled=True)  41.6 us
    psum x1, blocking collectives, shards(): lax.psum(jnp.sum(direction * applied), ('row', 'col'))  39.3 us
    all_to_all x3, blocking collectives, column_section(): lax.all_to_all(stacked, 'col', split_axis=1, concat_axis=2, tiled=True)  39 us
    ppermute x5, starting transfers between devices, padded(): lax.ppermute(lax.slice_in_dim(block, block.shape[dim] - width, None, axis...  22 us
    unnamed x146, local copies, waits for them, and re-layouts  20.6 us
    all_to_all x2, waiting for transfers between devices, column_section(): lax.all_to_all(result, 'col', split_axis=2, concat_axis=1, tiled=True)  17.1 us
  transfers between devices with their start and end apart: 14, of which 7 were waited for; matrix products, arithmetic and copies ran while one was open for 5% of the time, Pallas kernels for 0%

commit v1 on v0

v1 whole, which is shorter than its diff:
```python
import functools

import jax
import jax.numpy as jnp
from jax import lax
from jax.experimental import pallas as pl
from jax.experimental.pallas import tpu as pltpu
from jax.sharding import PartitionSpec as P

MESH = pl.DeviceIdType.MESH
BF16 = jnp.bfloat16
F32 = jnp.float32
OPS = 5


def dot(a, b):
    return jnp.dot(a, b, preferred_element_type=F32)


def prep_kernel(
    own_rows, own_cols, block,
    lcols, rcols, lblk, rblk,
    bf_ref, ba_ref, af_ref, aa_ref,
    lwin, rwin, lsem, rsem,
):
    nrb, ncb = lblk.shape[1], rblk.shape[1]
    row0 = lax.axis_index("row") * own_rows - 2
    col0 = lax.axis_index("col") * own_cols - 2

    def fetch(source, window, sem, first, total, factor, slot):
        at = jnp.clip(first + slot, 0, total - 1)
        return pltpu.make_async_copy(
            source.at[factor, at], window.at[factor, slot], sem.at[factor, slot]
        )

    copies = []
    for factor in range(2):
        for slot in range(own_cols + 4):
            copies.append(fetch(rblk, rwin, rsem, col0, ncb, factor, slot))
        for slot in range(own_rows + 4):
            copies.append(fetch(lblk, lwin, lsem, row0, nrb, factor, slot))
    for copy in copies:
        copy.start()
    for ref in (bf_ref, ba_ref, af_ref, aa_ref):
        ref[...] = jnp.zeros_like(ref)
    for copy in copies:
        copy.wait()

    for factor in range(2):
        for slot in range(own_cols + 4):
            at = col0 + slot
            inside = (at >= 0) & (at < ncb)
            safe = jnp.clip(at, 0, ncb - 1)
            for j in range(3):
                target = rcols[factor, safe, j] - col0
                own = target - 2

                @pl.when(inside & (own >= 0) & (own < own_cols))
                def _(factor=factor, slot=slot, j=j, own=own):
                    lanes = pl.ds(pl.multiple_of(own * block, block), block)
                    ba_ref[factor, pl.ds(slot * block, block), lanes] = rwin[factor, slot, j]

                if 2 <= slot < own_cols + 2:
                    rows = pl.ds(pl.multiple_of(target * block, block), block)
                    bf_ref[factor, rows, pl.ds((slot - 2) * block, block)] = rwin[
                        factor, slot, j
                    ].T
        for slot in range(own_rows + 4):
            at = row0 + slot
            inside = (at >= 0) & (at < nrb)
            safe = jnp.clip(at, 0, nrb - 1)
            for j in range(3):
                target = lcols[factor, safe, j] - row0
                own = target - 2

                @pl.when(inside & (own >= 0) & (own < own_rows))
                def _(factor=factor, slot=slot, j=j, own=own):
                    rows = pl.ds(pl.multiple_of(own * block, block), block)
                    aa_ref[factor, rows, pl.ds(slot * block, block)] = lwin[factor, slot, j].T

                if 2 <= slot < own_rows + 2:
                    lanes = pl.ds(pl.multiple_of(target * block, block), block)
                    af_ref[factor, pl.ds((slot - 2) * block, block), lanes] = lwin[
                        factor, slot, j
                    ]


def main_kernel(
    nrow, ncol, halo,
    weight_ref, meas_ref, den_ref, bf_ref, ba_ref, af_ref, aa_ref,
    sol_ref, res_ref,
    xo, xl, xr, wo, wu, wd, v0, v1, v2, stat, rstat, cstat,
    xsend, xrecv, wsend, wrecv, rsend, rrecv, csend, crecv,
):
    row = lax.axis_index("row")
    col = lax.axis_index("col")
    height, width = meas_ref.shape
    has_left, has_right = col > 0, col < ncol - 1
    has_up, has_down = row > 0, row < nrow - 1
    left, right = jnp.maximum(col - 1, 0), jnp.minimum(col + 1, ncol - 1)
    up, down = jnp.maximum(row - 1, 0), jnp.minimum(row + 1, nrow - 1)

    @pl.when(jnp.logical_not(has_left))
    def _():
        xl[...] = jnp.zeros_like(xl)

    @pl.when(jnp.logical_not(has_right))
    def _():
        xr[...] = jnp.zeros_like(xr)

    @pl.when(jnp.logical_not(has_up))
    def _():
        wu[...] = jnp.zeros_like(wu)

    @pl.when(jnp.logical_not(has_down))
    def _():
        wd[...] = jnp.zeros_like(wd)

    barrier = pltpu.get_barrier_semaphore()
    for step in range(1, nrow):
        pl.semaphore_signal(
            barrier, inc=1, device_id=(lax.rem(row + step, nrow), col), device_id_type=MESH
        )
    for step in range(1, ncol):
        pl.semaphore_signal(
            barrier, inc=1, device_id=(row, lax.rem(col + step, ncol)), device_id_type=MESH
        )
    pl.semaphore_wait(barrier, nrow + ncol - 2)

    def remote(src, dst, send, recv, device):
        return pltpu.make_async_remote_copy(
            src_ref=src, dst_ref=dst, send_sem=send, recv_sem=recv,
            device_id=device, device_id_type=MESH,
        )

    pending = []

    def operate(index, bmat, amat):
        to_right = remote(
            xo.at[index, :, pl.ds(width - halo, halo)], xl.at[index],
            xsend.at[index, 0], xrecv.at[index, 0], (row, right),
        )
        to_left = remote(
            xo.at[index, :, pl.ds(0, halo)], xr.at[index],
            xsend.at[index, 1], xrecv.at[index, 1], (row, left),
        )
        pl.when(has_right)(to_right.start)
        pl.when(has_left)(to_left.start)
        pending.append((has_right, to_right))
        pending.append((has_left, to_left))
        acc = [dot(xo[index], bmat[k, pl.ds(halo, width), :]) for k in range(2)]
        pl.when(has_left)(to_right.wait_recv)
        pl.when(has_right)(to_left.wait_recv)
        for k in range(2):
            total = acc[k] + dot(xl[index], bmat[k, pl.ds(0, halo), :])
            total = total + dot(xr[index], bmat[k, pl.ds(halo + width, halo), :])
            wo[index, k] = total.astype(BF16)
        to_down = remote(
            wo.at[index], wu.at[index], wsend.at[index, 0], wrecv.at[index, 0], (down, col)
        )
        to_up = remote(
            wo.at[index], wd.at[index], wsend.at[index, 1], wrecv.at[index, 1], (up, col)
        )
        pl.when(has_down)(to_down.start)
        pl.when(has_up)(to_up.start)
        pending.append((has_down, to_down))
        pending.append((has_up, to_up))
        out = dot(amat[0, :, pl.ds(halo, height)], wo[index, 0])
        out = out + dot(amat[1, :, pl.ds(halo, height)], wo[index, 1])
        pl.when(has_up)(to_down.wait_recv)
        pl.when(has_down)(to_up.wait_recv)
        for k in range(2):
            out = out + dot(amat[k, :, pl.ds(0, halo)], wu[index, k])
            out = out + dot(amat[k, :, pl.ds(halo + height, halo)], wd[index, k])
        return out

    weight = weight_ref[0]
    xo[0] = meas_ref[...].astype(BF16)
    first = operate(0, ba_ref, aa_ref) + weight * den_ref[...]
    v0[...] = first
    xo[1] = first.astype(BF16)
    xo[2] = operate(1, bf_ref, af_ref).astype(BF16)
    second = operate(2, ba_ref, aa_ref) + weight * v0[...]
    v1[...] = second
    xo[3] = second.astype(BF16)
    xo[4] = operate(3, bf_ref, af_ref).astype(BF16)
    v2[...] = operate(4, ba_ref, aa_ref) + weight * v1[...]

    def lanes(a, b):
        folded = jnp.sum(a[...] * b[...], axis=0, keepdims=True)
        total = folded[:, 0:128]
        for start in range(128, width, 128):
            total = total + folded[:, start : start + 128]
        return total

    for slot, (a, b) in enumerate(((v0, v0), (v0, v1), (v1, v1), (v0, v2), (v1, v2))):
        stat[0, pl.ds(slot, 1), :] = lanes(a, b)
    stat[0, pl.ds(5, 3), :] = jnp.zeros((3, 128), F32)

    def gather(source, slots, send, recv, count, device):
        copies = [
            remote(source, slots.at[step - 1], send.at[step - 1], recv.at[step - 1], device(step))
            for step in range(1, count)
        ]
        for copy in copies:
            copy.start()
        for copy in copies:
            copy.wait_recv()
        total = source[...]
        for step in range(1, count):
            total = total + slots[step - 1]
        for copy in copies:
            copy.wait_send()
        return total

    stat[1] = gather(
        stat.at[0], rstat, rsend, rrecv, nrow, lambda step: (lax.rem(row + step, nrow), col)
    )
    summed = gather(
        stat.at[1], cstat, csend, crecv, ncol, lambda step: (row, lax.rem(col + step, ncol))
    )
    grams = jnp.sum(summed, axis=1, keepdims=True)
    g00, g01, g11, g02, g12 = [grams[slot : slot + 1, :] for slot in range(5)]
    alpha = g00 / g01
    norm = alpha * alpha * g11 - 2.0 * alpha * g01 + g00
    beta = norm / (g00 + 1e-06)
    grow = 1.0 + beta
    curve = grow * grow * g01 - grow * alpha * (g02 + g11) + alpha * alpha * g12
    gamma = norm / curve
    sol_ref[...] = (alpha + gamma * grow) * v0[...] - (gamma * alpha) * v1[...]
    res_ref[...] = (
        v0[...] - (alpha + gamma * grow) * v1[...] + (gamma * alpha) * v2[...]
    )
    for condition, copy in pending:
        pl.when(condition)(copy.wait_send)


def shards(measured, denoised, reg_weight, left_blocks, left_cols, right_blocks, right_cols):
    block = left_blocks.shape[-1]
    height, width = measured.shape
    own_rows, own_cols = height // block, width // block
    nrow, ncol = lax.axis_size("row"), lax.axis_size("col")
    halo = 2 * block
    vmem = pl.BlockSpec(memory_space=pltpu.VMEM)
    smem = pl.BlockSpec(memory_space=pltpu.SMEM)
    hbm = pl.BlockSpec(memory_space=pl.ANY)
    wide, tall = width + 2 * halo, height + 2 * halo

    bf, ba, af, aa = pl.pallas_call(
        functools.partial(prep_kernel, own_rows, own_cols, block),
        out_shape=[
            jax.ShapeDtypeStruct((2, wide, width), BF16),
            jax.ShapeDtypeStruct((2, wide, width), BF16),
            jax.ShapeDtypeStruct((2, height, tall), BF16),
            jax.ShapeDtypeStruct((2, height, tall), BF16),
        ],
        in_specs=[smem, smem, hbm, hbm],
        out_specs=[vmem] * 4,
        scratch_shapes=[
            pltpu.VMEM((2, own_rows + 4, 3, block, block), BF16),
            pltpu.VMEM((2, own_cols + 4, 3, block, block), BF16),
            pltpu.SemaphoreType.DMA((2, own_rows + 4)),
            pltpu.SemaphoreType.DMA((2, own_cols + 4)),
        ],
        name="windows",
    )(left_cols, right_cols, left_blocks, right_blocks)

    dma = pltpu.SemaphoreType.DMA
    return pl.pallas_call(
        functools.partial(main_kernel, nrow, ncol, halo),
        out_shape=[jax.ShapeDtypeStruct((height, width), F32)] * 2,
        in_specs=[smem] + [vmem] * 6,
        out_specs=[vmem] * 2,
        scratch_shapes=[
            pltpu.VMEM((OPS, height, width), BF16),
            pltpu.VMEM((OPS, height, halo), BF16),
            pltpu.VMEM((OPS, height, halo), BF16),
            pltpu.VMEM((OPS, 2, height, width), BF16),
            pltpu.VMEM((OPS, 2, halo, width), BF16),
            pltpu.VMEM((OPS, 2, halo, width), BF16),
            pltpu.VMEM((height, width), F32),
            pltpu.VMEM((height, width), F32),
            pltpu.VMEM((height, width), F32),
            pltpu.VMEM((2, 8, 128), F32),
            pltpu.VMEM((nrow - 1, 8, 128), F32),
            pltpu.VMEM((ncol - 1, 8, 128), F32),
            dma((OPS, 2)), dma((OPS, 2)), dma((OPS, 2)), dma((OPS, 2)),
            dma((nrow - 1,)), dma((nrow - 1,)), dma((ncol - 1,)), dma((ncol - 1,)),
        ],
        compiler_params=pltpu.CompilerParams(
            collective_id=0, has_side_effects=True, vmem_limit_bytes=48 * 1024 * 1024
        ),
        name="conjugate",
    )(reg_weight, measured, denoised, bf, ba, af, aa)


def solution(mesh):
    return jax.shard_map(
        shards,
        mesh=mesh,
        in_specs=(P("row", "col"), P("row", "col"), P(), P(), P(), P(), P()),
        out_specs=(P("row", "col"), P("row", "col")),
        check_vma=False,
    )
```

time: 471 us -> 94.7 us (0.20); the launches traced: 465 us -> 94.4 us
  blocking collectives: 201 us -> 0 us
  Pallas kernels: 0 us -> 83.9 us
  other arithmetic: 81.6 us -> 0 us
  local copies, waits for them, and re-layouts: 69.2 us -> 9.17 us
  starting transfers between devices: 48.6 us -> 0 us
  matrix products: 29.6 us -> 0 us
  waiting for transfers between devices: 28.4 us -> 0 us
  between operations: 7.32 us -> 1.32 us
    psum x3 -> x0, blocking collectives: 120 us -> none  [the longest x2 80.7 us: global_squares(): return lax.psum(jnp.sum(values * values), ('row', 'col'))]
    pallas_call x0 -> x2, Pallas kernels: none -> 83.9 us  [the longest x1 75.9 us: shards(): pl.pallas_call(functools.partial(main_kernel, nrow, ncol, halo), out_shap...]
    all_to_all x6 -> x0, blocking collectives: 80.6 us -> none  [the longest x3 41.6 us: column_section(): lax.all_to_all(result, 'col', split_axis=2, concat_axis=1, tiled=True)]
    unnamed x5 -> x0, other arithmetic: 56.2 us -> none
    dot_general x20 -> x0, matrix products: 29.6 us -> none  [the longest x6 14.3 us: cols_adjoint(): jnp.einsum('rta,tjab->rtjb', margined, window, preferred_element_type=jnp...]
    ppermute x10 -> x0, starting transfers between devices: 28.5 us -> none  [the longest x5 22 us: padded(): lax.ppermute(lax.slice_in_dim(block, block.shape[dim] - width, None, axis...]
    all_to_all x4 -> x0, waiting for transfers between devices: 25 us -> none  [the longest x2 17.1 us: column_section(): lax.all_to_all(result, 'col', split_axis=2, concat_axis=1, tiled=True)]
    all_to_all x4 -> x0, starting transfers between devices: 20.2 us -> none  [the longest x2 10.8 us: column_section(): lax.all_to_all(stacked, 'col', split_axis=1, concat_axis=2, tiled=True)]
  transfers between devices with their start and end apart: 14 -> 0, of which waited for: 7 -> 0; matrix products, arithmetic and copies ran while one was open for 5% -> 0% of each run, Pallas kernels for 0% -> 0%
where the time goes in v1:
time: 94.7 us; the launch traced here: 94.4 us
  Pallas kernels  83.9 us (89%)
  local copies, waits for them, and re-layouts  9.17 us (10%)
  between operations  1.32 us (1%)
    pallas_call x1, Pallas kernels, shards(): pl.pallas_call(functools.partial(main_kernel, nrow, ncol, halo), out_shap...  75.9 us
    unnamed x16, local copies, waits for them, and re-layouts  9.17 us
    pallas_call x1, Pallas kernels, shards(): pl.pallas_call(functools.partial(prep_kernel, own_rows, own_cols, block),...  7.98 us

profile of v1, /device:TPU:0, one launch (start us, length us, event | category | flops | bytes accessed | tf_op | source)
XLA Modules:
  0.0 94.4 jit_solution(16627032786015608874)
XLA Ops:
  1.3 1.4 %copy.9.lcols = s32[2,8,3]{2,1,0:T(8,128)} copy(s32[2,8,3]{1,0,2:T(2,128)} %param.11) | data formatting | bytes 384 | tf_op args[4]
  2.6 1.4 %copy.10.rcols = s32[2,24,3]{2,1,0:T(8,128)} copy(s32[2,24,3]{1,0,2:T(2,128)} %param.13) | data formatting | bytes 1152 | tf_op args[6]
  4.0 0.0 copy-start.4
  4.0 0.0 copy-start.5
  4.0 8.0 %windows.1 = (bf16[2,896,384]{2,1,0:T(8,128)(2,1)}, bf16[2,896,384]{2,1,0:T(8,128)(2,1)}, bf16[2,256,768]{2,1,0:T(8,128)(2,1)}, bf16[2,256,768]{2,1,0:T(8,128)(2,1)}) custom-call(s32[2,8,3]{2,1,0:T(8,128)} %copy.9.lcols, s32[2,24,3]{2,1,0:T(8,128)} %copy.10.rcols, bf16[2,8,3,128,128]{4,3,2,1,0:T(8,128)(2,1)} %lblk.1, bf16[2,24,3,128,128]{4,3,2,1,0:T(8,128)(2,1)} %rblk.1), custom_call_target="tpu_custom_call" | custom-call | tf_op jit(solution)/shard_map/windows/pallas_call | solution.py:249
  12.0 0.0 copy-done.4
  12.0 0.0 copy-done.5
  12.0 0.0 copy-start
  12.0 1.3 %copy-done = bf16[2,896,384]{2,1,0:T(8,128)(2,1)S(1)} copy-done((bf16[2,896,384]{2,1,0:T(8,128)(2,1)S(1)}, bf16[2,896,384]{2,1,0:T(8,128)(2,1)}, u32[]{:S(2)}) %copy-start) | copy-done | bytes 1376280
  13.4 0.0 copy-start.1
  13.4 1.3 %copy-done.1 = bf16[2,896,384]{2,1,0:T(8,128)(2,1)S(1)} copy-done((bf16[2,896,384]{2,1,0:T(8,128)(2,1)S(1)}, bf16[2,896,384]{2,1,0:T(8,128)(2,1)}, u32[]{:S(2)}) %copy-start.1) | copy-done | bytes 1376280
  14.7 0.0 copy-start.2
  14.7 1.1 %copy-done.2 = bf16[2,256,768]{2,1,0:T(8,128)(2,1)S(1)} copy-done((bf16[2,256,768]{2,1,0:T(8,128)(2,1)S(1)}, bf16[2,256,768]{2,1,0:T(8,128)(2,1)}, u32[]{:S(2)}) %copy-start.2) | copy-done | bytes 786456
  15.8 0.0 copy-start.3
  15.8 1.1 %copy-done.3 = bf16[2,256,768]{2,1,0:T(8,128)(2,1)S(1)} copy-done((bf16[2,256,768]{2,1,0:T(8,128)(2,1)S(1)}, bf16[2,256,768]{2,1,0:T(8,128)(2,1)}, u32[]{:S(2)}) %copy-start.3) | copy-done | bytes 786456
  17.0 75.9 %conjugate.1 = (f32[256,384]{1,0:T(8,128)S(1)}, f32[256,384]{1,0:T(8,128)S(1)}) custom-call(f32[1]{0:T(128)S(6)} %copy.13.weight_ref, f32[256,384]{1,0:T(8,128)S(1)} %copy-done.4, f32[256,384]{1,0:T(8,128)S(1)} %copy-done.5, bf16[2,896,384]{2,1,0:T(8,128)(2,1)S(1)} %copy-done, bf16[2,896,384]{2,1,0:T(8,128)(2,1)S(1)} %copy-done.1, ...), custom_call_target="tpu_custom_call" | custom-call | tf_op jit(solution)/shard_map/conjugate/pallas_call | solution.py:269
  92.9 0.7 copy.14
  93.6 0.7 copy.15
Async XLA Ops:
  4.0 8.0 %copy-start.4 = (f32[256,384]{1,0:T(8,128)S(1)}, f32[256,384]{1,0:T(8,128)}, u32[]{:S(2)}) copy-start(f32[256,384]{1,0:T(8,128)} %meas_ref.1) | copy-start | bytes 1179652
  4.0 8.0 %copy-start.5 = (f32[256,384]{1,0:T(8,128)S(1)}, f32[256,384]{1,0:T(8,128)}, u32[]{:S(2)}) copy-start(f32[256,384]{1,0:T(8,128)} %den_ref.1) | copy-start | bytes 1179652
  12.0 1.3 %copy-start = (bf16[2,896,384]{2,1,0:T(8,128)(2,1)S(1)}, bf16[2,896,384]{2,1,0:T(8,128)(2,1)}, u32[]{:S(2)}) copy-start(bf16[2,896,384]{2,1,0:T(8,128)(2,1)} %get-tuple-element.6.bf_ref) | copy-start | bytes 4128772
  13.4 1.3 %copy-start.1 = (bf16[2,896,384]{2,1,0:T(8,128)(2,1)S(1)}, bf16[2,896,384]{2,1,0:T(8,128)(2,1)}, u32[]{:S(2)}) copy-start(bf16[2,896,384]{2,1,0:T(8,128)(2,1)} %get-tuple-element.7.ba_ref) | copy-start | bytes 4128772
  14.7 1.1 %copy-start.2 = (bf16[2,256,768]{2,1,0:T(8,128)(2,1)S(1)}, bf16[2,256,768]{2,1,0:T(8,128)(2,1)}, u32[]{:S(2)}) copy-start(bf16[2,256,768]{2,1,0:T(8,128)(2,1)} %get-tuple-element.8.af_ref) | copy-start | bytes 2359300
  15.8 1.1 %copy-start.3 = (bf16[2,256,768]{2,1,0:T(8,128)(2,1)S(1)}, bf16[2,256,768]{2,1,0:T(8,128)(2,1)}, u32[]{:S(2)}) copy-start(bf16[2,256,768]{2,1,0:T(8,128)(2,1)} %get-tuple-element.9.aa_ref) | copy-start | bytes 2359300

commit v2 on v1

v2 whole, which is shorter than its diff:
```python
import functools

import jax
import jax.numpy as jnp
from jax import lax
from jax.experimental import pallas as pl
from jax.experimental.pallas import tpu as pltpu
from jax.sharding import PartitionSpec as P

MESH = pl.DeviceIdType.MESH
BF16 = jnp.bfloat16
F32 = jnp.float32
OPS = 5


def dot(a, b):
    return jnp.dot(a, b, preferred_element_type=F32)


def main_kernel(
    nrow, ncol, block,
    weight_ref, lcols, rcols, meas_hbm, den_hbm, lblk, rblk,
    sol_ref, res_ref,
    meas, den, lwin, rwin, bf_ref, ba_ref, af_ref, aa_ref,
    xo, xl, xr, wo, wu, wd, v0, v1, v2, stat, rstat, cstat,
    msem, lsem, rsem, xsend, xrecv, wsend, wrecv, rsend, rrecv, csend, crecv,
):
    row = lax.axis_index("row")
    col = lax.axis_index("col")
    height, width = meas.shape
    halo = 2 * block
    own_rows, own_cols = height // block, width // block
    nrb, ncb = lblk.shape[1], rblk.shape[1]
    row0, col0 = row * own_rows - 2, col * own_cols - 2
    has_left, has_right = col > 0, col < ncol - 1
    has_up, has_down = row > 0, row < nrow - 1
    left, right = jnp.maximum(col - 1, 0), jnp.minimum(col + 1, ncol - 1)
    up, down = jnp.maximum(row - 1, 0), jnp.minimum(row + 1, nrow - 1)

    load_meas = pltpu.make_async_copy(meas_hbm, meas, msem.at[0])
    load_den = pltpu.make_async_copy(den_hbm, den, msem.at[1])
    load_meas.start()

    def fetch(source, window, sem, first, total, count):
        return [
            pltpu.make_async_copy(
                source.at[k, jnp.clip(first + t, 0, total - 1)], window.at[k, t], sem.at[k, t]
            )
            for k in range(2)
            for t in range(count)
        ]

    load_right = fetch(rblk, rwin, rsem, col0, ncb, own_cols + 4)
    load_left = fetch(lblk, lwin, lsem, row0, nrb, own_rows + 4)
    for copy in load_right:
        copy.start()
    for copy in load_left:
        copy.start()
    load_den.start()

    barrier = pltpu.get_barrier_semaphore()

    @pl.when(jnp.logical_not(has_left))
    def _():
        xl[...] = jnp.zeros_like(xl)

    @pl.when(jnp.logical_not(has_right))
    def _():
        xr[...] = jnp.zeros_like(xr)

    @pl.when(jnp.logical_not(has_up))
    def _():
        wu[...] = jnp.zeros_like(wu)

    @pl.when(jnp.logical_not(has_down))
    def _():
        wd[...] = jnp.zeros_like(wd)

    for step in range(1, nrow):
        pl.semaphore_signal(
            barrier, inc=1, device_id=(lax.rem(row + step, nrow), col), device_id_type=MESH
        )
    for step in range(1, ncol):
        pl.semaphore_signal(
            barrier, inc=1, device_id=(row, lax.rem(col + step, ncol)), device_id_type=MESH
        )
    load_meas.wait()
    xo[0] = meas[...].astype(BF16)
    pl.semaphore_wait(barrier, nrow + ncol - 2)

    def remote(src, dst, send, recv, device):
        return pltpu.make_async_remote_copy(
            src_ref=src, dst_ref=dst, send_sem=send, recv_sem=recv,
            device_id=device, device_id_type=MESH,
        )

    def hit(cols, k, at, total, j, wanted):
        inside = (at >= 0) & (at < total)
        same = cols[k, jnp.clip(at, 0, total - 1), j] == wanted
        return jnp.where(inside & same, 1.0, 0.0).astype(F32)

    def mixed(sources, weights):
        total = sources[0] * weights[0]
        for source, factor in zip(sources[1:], weights[1:]):
            total = total + source * factor
        return total

    def span(index):
        return pl.ds(index * block, block)

    empty = jnp.zeros((block, block), BF16)

    def build_ba():
        for copy in load_right:
            copy.wait()
        for k in range(2):
            for t in range(own_cols + 4):
                sources = [rwin[k, t, j].astype(F32) for j in range(3)]
                for c in range(own_cols):
                    if c <= t <= c + 4:
                        weights = [
                            hit(rcols, k, col0 + t, ncb, j, col0 + 2 + c) for j in range(3)
                        ]
                        ba_ref[k, span(t), span(c)] = mixed(sources, weights).astype(BF16)
                    else:
                        ba_ref[k, span(t), span(c)] = empty

    def build_bf():
        for k in range(2):
            for c in range(own_cols):
                sources = [rwin[k, c + 2, j].astype(F32).T for j in range(3)]
                for t in range(own_cols + 4):
                    if c <= t <= c + 4:
                        weights = [
                            hit(rcols, k, col0 + 2 + c, ncb, j, col0 + t) for j in range(3)
                        ]
                        bf_ref[k, span(t), span(c)] = mixed(sources, weights).astype(BF16)
                    else:
                        bf_ref[k, span(t), span(c)] = empty

    def build_aa():
        for copy in load_left:
            copy.wait()
        for k in range(2):
            for t in range(own_rows + 4):
                sources = [lwin[k, t, j].astype(F32) for j in range(3)]
                for r in range(own_rows):
                    if r <= t <= r + 4:
                        weights = [
                            hit(lcols, k, row0 + t, nrb, j, row0 + 2 + r) for j in range(3)
                        ]
                        aa_ref[k, span(r), span(t)] = mixed(sources, weights).T.astype(BF16)
                    else:
                        aa_ref[k, span(r), span(t)] = empty

    def build_af():
        for k in range(2):
            for r in range(own_rows):
                sources = [lwin[k, r + 2, j].astype(F32) for j in range(3)]
                for t in range(own_rows + 4):
                    if r <= t <= r + 4:
                        weights = [
                            hit(lcols, k, row0 + 2 + r, nrb, j, row0 + t) for j in range(3)
                        ]
                        af_ref[k, span(r), span(t)] = mixed(sources, weights).astype(BF16)
                    else:
                        af_ref[k, span(r), span(t)] = empty

    pending = []
    chunks = range(own_rows)

    def operate(index, bmat, amat, fill_b=None, fill_a=None):
        sides = []
        for q in chunks:
            to_right = remote(
                xo.at[index, span(q), pl.ds(width - halo, halo)], xl.at[index, span(q)],
                xsend.at[index, q, 0], xrecv.at[index, q, 0], (row, right),
            )
            to_left = remote(
                xo.at[index, span(q), pl.ds(0, halo)], xr.at[index, span(q)],
                xsend.at[index, q, 1], xrecv.at[index, q, 1], (row, left),
            )
            pl.when(has_right)(to_right.start)
            pl.when(has_left)(to_left.start)
            pending.append((has_right, to_right))
            pending.append((has_left, to_left))
            sides.append((to_right, to_left))
        if fill_b is not None:
            fill_b()
        acc = [dot(xo[index], bmat[k, pl.ds(halo, width), :]) for k in range(2)]
        ends = []
        for q in chunks:
            to_right, to_left = sides[q]
            pl.when(has_left)(to_right.wait_recv)
            pl.when(has_right)(to_left.wait_recv)
            for k in range(2):
                total = acc[k][q * block : (q + 1) * block]
                total = total + dot(xl[index, span(q)], bmat[k, pl.ds(0, halo), :])
                total = total + dot(xr[index, span(q)], bmat[k, pl.ds(halo + width, halo), :])
                wo[index, q, k] = total.astype(BF16)
            to_down = remote(
                wo.at[index, q], wu.at[index, q],
                wsend.at[index, q, 0], wrecv.at[index, q, 0], (down, col),
            )
            to_up = remote(
                wo.at[index, q], wd.at[index, q],
                wsend.at[index, q, 1], wrecv.at[index, q, 1], (up, col),
            )
            pl.when(has_down)(to_down.start)
            pl.when(has_up)(to_up.start)
            pending.append((has_down, to_down))
            pending.append((has_up, to_up))
            ends.append((to_down, to_up))
        if fill_a is not None:
            fill_a()

        def part(products, first):
            sums = [
                dot(
                    amat[k, :, pl.ds(first * block, height)],
                    jnp.concatenate([products[index, q, k] for q in chunks], axis=0),
                )
                for k in range(2)
            ]
            return sums[0] + sums[1]

        out = part(wo, 2)
        for q in chunks:
            to_down, to_up = ends[q]
            pl.when(has_up)(to_down.wait_recv)
            pl.when(has_down)(to_up.wait_recv)
        return out + part(wu, 0) + part(wd, 2 + own_rows)

    weight = weight_ref[0]
    first = operate(0, ba_ref, aa_ref, build_ba, build_aa)
    load_den.wait()
    first = first + weight * den[...]
    xo[1] = first.astype(BF16)
    v0[...] = first
    xo[2] = operate(1, bf_ref, af_ref, build_bf, build_af).astype(BF16)
    second = operate(2, ba_ref, aa_ref) + weight * v0[...]
    xo[3] = second.astype(BF16)
    v1[...] = second
    xo[4] = operate(3, bf_ref, af_ref).astype(BF16)
    v2[...] = operate(4, ba_ref, aa_ref) + weight * v1[...]

    def lanes(a, b):
        folded = jnp.sum(a[...] * b[...], axis=0, keepdims=True)
        total = folded[:, 0:128]
        for start in range(128, width, 128):
            total = total + folded[:, start : start + 128]
        return total

    for slot, (a, b) in enumerate(((v0, v0), (v0, v1), (v1, v1), (v0, v2), (v1, v2))):
        stat[0, pl.ds(slot, 1), :] = lanes(a, b)
    stat[0, pl.ds(5, 3), :] = jnp.zeros((3, 128), F32)

    def gather(source, slots, send, recv, count, device):
        copies = [
            remote(source, slots.at[step - 1], send.at[step - 1], recv.at[step - 1], device(step))
            for step in range(1, count)
        ]
        for copy in copies:
            copy.start()
        for copy in copies:
            copy.wait_recv()
        total = source[...]
        for step in range(1, count):
            total = total + slots[step - 1]
        for copy in copies:
            copy.wait_send()
        return total

    stat[1] = gather(
        stat.at[0], rstat, rsend, rrecv, nrow, lambda step: (lax.rem(row + step, nrow), col)
    )
    summed = gather(
        stat.at[1], cstat, csend, crecv, ncol, lambda step: (row, lax.rem(col + step, ncol))
    )
    grams = jnp.sum(summed, axis=1, keepdims=True)
    g00, g01, g11, g02, g12 = [grams[slot : slot + 1, :] for slot in range(5)]
    alpha = g00 / g01
    norm = alpha * alpha * g11 - 2.0 * alpha * g01 + g00
    beta = norm / (g00 + 1e-06)
    grow = 1.0 + beta
    curve = grow * grow * g01 - grow * alpha * (g02 + g11) + alpha * alpha * g12
    gamma = norm / curve
    sol_ref[...] = (alpha + gamma * grow) * v0[...] - (gamma * alpha) * v1[...]
    res_ref[...] = (
        v0[...] - (alpha + gamma * grow) * v1[...] + (gamma * alpha) * v2[...]
    )
    for condition, copy in pending:
        pl.when(condition)(copy.wait_send)


def shards(measured, denoised, reg_weight, left_blocks, left_cols, right_blocks, right_cols):
    block = left_blocks.shape[-1]
    height, width = measured.shape
    own_rows, own_cols = height // block, width // block
    nrow, ncol = lax.axis_size("row"), lax.axis_size("col")
    halo = 2 * block
    smem = pl.BlockSpec(memory_space=pltpu.SMEM)
    hbm = pl.BlockSpec(memory_space=pl.ANY)
    wide, tall = width + 2 * halo, height + 2 * halo
    field = pltpu.VMEM((height, width), F32)
    dma = pltpu.SemaphoreType.DMA
    return pl.pallas_call(
        functools.partial(main_kernel, nrow, ncol, block),
        out_shape=[jax.ShapeDtypeStruct((height, width), F32)] * 2,
        in_specs=[smem] * 3 + [hbm] * 4,
        out_specs=[pl.BlockSpec(memory_space=pltpu.VMEM)] * 2,
        scratch_shapes=[
            field,
            field,
            pltpu.VMEM((2, own_rows + 4, 3, block, block), BF16),
            pltpu.VMEM((2, own_cols + 4, 3, block, block), BF16),
            pltpu.VMEM((2, wide, width), BF16),
            pltpu.VMEM((2, wide, width), BF16),
            pltpu.VMEM((2, height, tall), BF16),
            pltpu.VMEM((2, height, tall), BF16),
            pltpu.VMEM((OPS, height, width), BF16),
            pltpu.VMEM((OPS, height, halo), BF16),
            pltpu.VMEM((OPS, height, halo), BF16),
            pltpu.VMEM((OPS, own_rows, 2, block, width), BF16),
            pltpu.VMEM((OPS, own_rows, 2, block, width), BF16),
            pltpu.VMEM((OPS, own_rows, 2, block, width), BF16),
            field,
            field,
            field,
            pltpu.VMEM((2, 8, 128), F32),
            pltpu.VMEM((nrow - 1, 8, 128), F32),
            pltpu.VMEM((ncol - 1, 8, 128), F32),
            dma((2,)), dma((2, own_rows + 4)), dma((2, own_cols + 4)),
            dma((OPS, own_rows, 2)), dma((OPS, own_rows, 2)),
            dma((OPS, own_rows, 2)), dma((OPS, own_rows, 2)),
            dma((nrow - 1,)), dma((nrow - 1,)), dma((ncol - 1,)), dma((ncol - 1,)),
        ],
        compiler_params=pltpu.CompilerParams(
            collective_id=0, has_side_effects=True, vmem_limit_bytes=48 * 1024 * 1024
        ),
        name="conjugate",
    )(reg_weight, left_cols, right_cols, measured, denoised, left_blocks, right_blocks)


def solution(mesh):
    return jax.shard_map(
        shards,
        mesh=mesh,
        in_specs=(P("row", "col"), P("row", "col"), P(), P(), P(), P(), P()),
        out_specs=(P("row", "col"), P("row", "col")),
        check_vma=False,
    )
```

time: 94.7 us -> 81.4 us (0.86)
  Pallas kernels: 83.9 us -> 73.4 us
  local copies, waits for them, and re-layouts: 9.17 us -> 6.43 us
    pallas_call x2 -> x1, Pallas kernels: 83.9 us -> 73.4 us  [shards(): pl.pallas_call(functools.partial(main_kernel, nrow, ncol, block), out_sha...]
    unnamed x16 -> x10, local copies, waits for them, and re-layouts: 9.17 us -> 6.43 us
where the time goes in v2:
time: 81.4 us; the launch traced here: 81.1 us
  Pallas kernels  73.4 us (90%)
  local copies, waits for them, and re-layouts  6.43 us (8%)
  between operations  1.29 us (2%)
    pallas_call x1, Pallas kernels, shards(): pl.pallas_call(functools.partial(main_kernel, nrow, ncol, block), out_sha...  73.4 us
    unnamed x10, local copies, waits for them, and re-layouts  6.43 us

profile of v2, /device:TPU:0, one launch (start us, length us, event | category | flops | bytes accessed | tf_op | source)
XLA Modules:
  0.0 81.1 jit_solution(7742388753130174040)
XLA Ops:
  1.3 0.8 copy.9.lcols
  2.0 0.8 copy.10.rcols
  2.8 0.0 copy-start
  2.8 1.4 %copy-done = bf16[2,8,3,128,128]{4,3,2,1,0:T(8,128)(2,1)S(1)} copy-done((bf16[2,8,3,128,128]{4,3,2,1,0:T(8,128)(2,1)S(1)}, bf16[2,8,3,128,128]{4,3,2,1,0:T(8,128)(2,1)}, u32[]{:S(2)}) %copy-start) | copy-done | bytes 1572888
  4.2 0.0 copy-start.1
  4.2 1.0 %copy-done.1 = f32[256,384]{1,0:T(8,128)S(1)} copy-done((f32[256,384]{1,0:T(8,128)S(1)}, f32[256,384]{1,0:T(8,128)}, u32[]{:S(2)}) %copy-start.1) | copy-done | bytes 393240
  5.2 0.0 copy-start.2
  5.2 1.0 %copy-done.2 = f32[256,384]{1,0:T(8,128)S(1)} copy-done((f32[256,384]{1,0:T(8,128)S(1)}, f32[256,384]{1,0:T(8,128)}, u32[]{:S(2)}) %copy-start.2) | copy-done | bytes 393240
  6.2 73.4 %conjugate.1 = (f32[256,384]{1,0:T(8,128)S(1)}, f32[256,384]{1,0:T(8,128)S(1)}) custom-call(f32[1]{0:T(128)S(6)} %copy.13.weight_ref, s32[2,8,3]{2,1,0:T(8,128)S(1)} %copy.9.lcols, s32[2,24,3]{2,1,0:T(8,128)S(1)} %copy.10.rcols, f32[256,384]{1,0:T(8,128)S(1)} %copy-done.1, f32[256,384]{1,0:T(8,128)S(1)} %copy-done.2, ...), custom_call_target="tpu_custom_call" | custom-call | tf_op jit(solution)/shard_map/conjugate/pallas_call | solution.py:307
  79.6 0.7 copy.14
  80.3 0.7 copy.15
Async XLA Ops:
  2.8 1.4 %copy-start = (bf16[2,8,3,128,128]{4,3,2,1,0:T(8,128)(2,1)S(1)}, bf16[2,8,3,128,128]{4,3,2,1,0:T(8,128)(2,1)}, u32[]{:S(2)}) copy-start(bf16[2,8,3,128,128]{4,3,2,1,0:T(8,128)(2,1)} %lblk.1) | copy-start | bytes 4718596
  4.2 1.0 %copy-start.1 = (f32[256,384]{1,0:T(8,128)S(1)}, f32[256,384]{1,0:T(8,128)}, u32[]{:S(2)}) copy-start(f32[256,384]{1,0:T(8,128)} %meas_hbm.1) | copy-start | bytes 1179652
  5.2 1.0 %copy-start.2 = (f32[256,384]{1,0:T(8,128)S(1)}, f32[256,384]{1,0:T(8,128)}, u32[]{:S(2)}) copy-start(f32[256,384]{1,0:T(8,128)} %den_hbm.1) | copy-start | bytes 1179652

commit v3 on v2

--- a/solution.py
+++ b/solution.py
@@ -22,7 +22,7 @@
     weight_ref, lcols, rcols, meas_hbm, den_hbm, lblk, rblk,
     sol_ref, res_ref,
     meas, den, lwin, rwin, bf_ref, ba_ref, af_ref, aa_ref,
-    xo, xl, xr, wo, wu, wd, v0, v1, v2, stat, rstat, cstat,
+    xo, xl, xr, wo, pu, pd, ru, rd, v0, v1, v2, stat, rstat, cstat,
     msem, lsem, rsem, xsend, xrecv, wsend, wrecv, rsend, rrecv, csend, crecv,
 ):
     row = lax.axis_index("row")
@@ -70,11 +70,11 @@
 
     @pl.when(jnp.logical_not(has_up))
     def _():
-        wu[...] = jnp.zeros_like(wu)
+        ru[...] = jnp.zeros_like(ru)
 
     @pl.when(jnp.logical_not(has_down))
     def _():
-        wd[...] = jnp.zeros_like(wd)
+        rd[...] = jnp.zeros_like(rd)
 
     for step in range(1, nrow):
         pl.semaphore_signal(
@@ -142,6 +142,20 @@
         for copy in load_left:
             copy.wait()
         for k in range(2):
+            for r in range(own_rows):
+                sources = [lwin[k, r + 2, j].astype(F32).T for j in range(3)]
+                for t in range(own_rows + 4):
+                    if r <= t <= r + 4:
+                        weights = [
+                            hit(lcols, k, row0 + 2 + r, nrb, j, row0 + t) for j in range(3)
+                        ]
+                        value = mixed(sources, weights).astype(BF16)
+                    else:
+                        value = empty
+                    aa_ref[span(t), span(k * own_rows + r)] = value
+
+    def build_af():
+        for k in range(2):
             for t in range(own_rows + 4):
                 sources = [lwin[k, t, j].astype(F32) for j in range(3)]
                 for r in range(own_rows):
@@ -149,22 +163,10 @@
                         weights = [
                             hit(lcols, k, row0 + t, nrb, j, row0 + 2 + r) for j in range(3)
                         ]
-                        aa_ref[k, span(r), span(t)] = mixed(sources, weights).T.astype(BF16)
+                        value = mixed(sources, weights).astype(BF16)
                     else:
-                        aa_ref[k, span(r), span(t)] = empty
-
-    def build_af():
-        for k in range(2):
-            for r in range(own_rows):
-                sources = [lwin[k, r + 2, j].astype(F32) for j in range(3)]
-                for t in range(own_rows + 4):
-                    if r <= t <= r + 4:
-                        weights = [
-                            hit(lcols, k, row0 + 2 + r, nrb, j, row0 + t) for j in range(3)
-                        ]
-                        af_ref[k, span(r), span(t)] = mixed(sources, weights).astype(BF16)
-                    else:
-                        af_ref[k, span(r), span(t)] = empty
+                        value = empty
+                    af_ref[span(t), span(k * own_rows + r)] = value
 
     pending = []
     chunks = range(own_rows)
@@ -188,7 +190,6 @@
         if fill_b is not None:
             fill_b()
         acc = [dot(xo[index], bmat[k, pl.ds(halo, width), :]) for k in range(2)]
-        ends = []
         for q in chunks:
             to_right, to_left = sides[q]
             pl.when(has_left)(to_right.wait_recv)
@@ -197,39 +198,26 @@
                 total = acc[k][q * block : (q + 1) * block]
                 total = total + dot(xl[index, span(q)], bmat[k, pl.ds(0, halo), :])
                 total = total + dot(xr[index, span(q)], bmat[k, pl.ds(halo + width, halo), :])
-                wo[index, q, k] = total.astype(BF16)
-            to_down = remote(
-                wo.at[index, q], wu.at[index, q],
-                wsend.at[index, q, 0], wrecv.at[index, q, 0], (down, col),
-            )
-            to_up = remote(
-                wo.at[index, q], wd.at[index, q],
-                wsend.at[index, q, 1], wrecv.at[index, q, 1], (up, col),
-            )
-            pl.when(has_down)(to_down.start)
-            pl.when(has_up)(to_up.start)
-            pending.append((has_down, to_down))
-            pending.append((has_up, to_up))
-            ends.append((to_down, to_up))
+                wo[span(k * own_rows + q)] = total.astype(BF16)
         if fill_a is not None:
             fill_a()
-
-        def part(products, first):
-            sums = [
-                dot(
-                    amat[k, :, pl.ds(first * block, height)],
-                    jnp.concatenate([products[index, q, k] for q in chunks], axis=0),
-                )
-                for k in range(2)
-            ]
-            return sums[0] + sums[1]
-
-        out = part(wo, 2)
-        for q in chunks:
-            to_down, to_up = ends[q]
-            pl.when(has_up)(to_down.wait_recv)
-            pl.when(has_down)(to_up.wait_recv)
-        return out + part(wu, 0) + part(wd, 2 + own_rows)
+        products = wo[...]
+        to_down = remote(
+            pd.at[index], ru.at[index], wsend.at[index, 0], wrecv.at[index, 0], (down, col)
+        )
+        to_up = remote(
+            pu.at[index], rd.at[index], wsend.at[index, 1], wrecv.at[index, 1], (up, col)
+        )
+        pd[index] = dot(amat[pl.ds(halo + height, halo), :], products).astype(BF16)
+        pl.when(has_down)(to_down.start)
+        pu[index] = dot(amat[pl.ds(0, halo), :], products).astype(BF16)
+        pl.when(has_up)(to_up.start)
+        pending.append((has_down, to_down))
+        pending.append((has_up, to_up))
+        out = dot(amat[pl.ds(halo, height), :], products)
+        pl.when(has_up)(to_down.wait_recv)
+        pl.when(has_down)(to_up.wait_recv)
+        return out + ru[index].astype(F32) + rd[index].astype(F32)
 
     weight = weight_ref[0]
     first = operate(0, ba_ref, aa_ref, build_ba, build_aa)
@@ -300,7 +288,7 @@
     nrow, ncol = lax.axis_size("row"), lax.axis_size("col")
     halo = 2 * block
     smem = pl.BlockSpec(memory_space=pltpu.SMEM)
-    hbm = pl.BlockSpec(memory_space=pl.ANY)
+    hbm = pl.BlockSpec(memory_space=pltpu.HBM)
     wide, tall = width + 2 * halo, height + 2 * halo
     field = pltpu.VMEM((height, width), F32)
     dma = pltpu.SemaphoreType.DMA
@@ -316,14 +304,16 @@
             pltpu.VMEM((2, own_cols + 4, 3, block, block), BF16),
             pltpu.VMEM((2, wide, width), BF16),
             pltpu.VMEM((2, wide, width), BF16),
-            pltpu.VMEM((2, height, tall), BF16),
-            pltpu.VMEM((2, height, tall), BF16),
+            pltpu.VMEM((tall, 2 * height), BF16),
+            pltpu.VMEM((tall, 2 * height), BF16),
             pltpu.VMEM((OPS, height, width), BF16),
             pltpu.VMEM((OPS, height, halo), BF16),
             pltpu.VMEM((OPS, height, halo), BF16),
-            pltpu.VMEM((OPS, own_rows, 2, block, width), BF16),
-            pltpu.VMEM((OPS, own_rows, 2, block, width), BF16),
-            pltpu.VMEM((OPS, own_rows, 2, block, width), BF16),
+            pltpu.VMEM((2 * height, width), BF16),
+            pltpu.VMEM((OPS, halo, width), BF16),
+            pltpu.VMEM((OPS, halo, width), BF16),
+            pltpu.VMEM((OPS, halo, width), BF16),
+            pltpu.VMEM((OPS, halo, width), BF16),
             field,
             field,
             field,
@@ -332,7 +322,7 @@
             pltpu.VMEM((ncol - 1, 8, 128), F32),
             dma((2,)), dma((2, own_rows + 4)), dma((2, own_cols + 4)),
             dma((OPS, own_rows, 2)), dma((OPS, own_rows, 2)),
-            dma((OPS, own_rows, 2)), dma((OPS, own_rows, 2)),
+            dma((OPS, 2)), dma((OPS, 2)),
             dma((nrow - 1,)), dma((nrow - 1,)), dma((ncol - 1,)), dma((ncol - 1,)),
         ],
         compiler_params=pltpu.CompilerParams(

time: 81.4 us -> 77.2 us (0.948)
  Pallas kernels: 73.4 us -> 69.2 us
    pallas_call x1, Pallas kernels: 73.4 us -> 69.2 us  [shards(): pl.pallas_call(functools.partial(main_kernel, nrow, ncol, block), out_sha...]
where the time goes in v3:
time: 77.2 us; the launch traced here: 76.9 us
  Pallas kernels  69.2 us (90%)
  local copies, waits for them, and re-layouts  6.43 us (8%)
  between operations  1.29 us (2%)
    pallas_call x1, Pallas kernels, shards(): pl.pallas_call(functools.partial(main_kernel, nrow, ncol, block), out_sha...  69.2 us
    unnamed x10, local copies, waits for them, and re-layouts  6.43 us

profile of v3, /device:TPU:0, one launch (start us, length us, event | category | flops | bytes accessed | tf_op | source)
XLA Modules:
  0.0 76.9 jit_solution(11122914740647908697)
XLA Ops:
  1.3 0.8 copy.9.lcols
  2.0 0.8 copy.10.rcols
  2.8 0.0 copy-start
  2.8 1.4 %copy-done = bf16[2,8,3,128,128]{4,3,2,1,0:T(8,128)(2,1)S(1)} copy-done((bf16[2,8,3,128,128]{4,3,2,1,0:T(8,128)(2,1)S(1)}, bf16[2,8,3,128,128]{4,3,2,1,0:T(8,128)(2,1)}, u32[]{:S(2)}) %copy-start) | copy-done | bytes 1572888
  4.2 0.0 copy-start.1
  4.2 1.0 %copy-done.1 = f32[256,384]{1,0:T(8,128)S(1)} copy-done((f32[256,384]{1,0:T(8,128)S(1)}, f32[256,384]{1,0:T(8,128)}, u32[]{:S(2)}) %copy-start.1) | copy-done | bytes 393240
  5.2 0.0 copy-start.2
  5.2 1.0 %copy-done.2 = f32[256,384]{1,0:T(8,128)S(1)} copy-done((f32[256,384]{1,0:T(8,128)S(1)}, f32[256,384]{1,0:T(8,128)}, u32[]{:S(2)}) %copy-start.2) | copy-done | bytes 393240
  6.2 69.2 %conjugate.1 = (f32[256,384]{1,0:T(8,128)S(1)}, f32[256,384]{1,0:T(8,128)S(1)}) custom-call(f32[1]{0:T(128)S(6)} %copy.13.weight_ref, s32[2,8,3]{2,1,0:T(8,128)S(1)} %copy.9.lcols, s32[2,24,3]{2,1,0:T(8,128)S(1)} %copy.10.rcols, f32[256,384]{1,0:T(8,128)S(1)} %copy-done.1, f32[256,384]{1,0:T(8,128)S(1)} %copy-done.2, ...), custom_call_target="tpu_custom_call" | custom-call | tf_op jit(solution)/shard_map/conjugate/pallas_call | solution.py:295
  75.4 0.7 copy.14
  76.2 0.7 copy.15
Async XLA Ops:
  2.8 1.4 %copy-start = (bf16[2,8,3,128,128]{4,3,2,1,0:T(8,128)(2,1)S(1)}, bf16[2,8,3,128,128]{4,3,2,1,0:T(8,128)(2,1)}, u32[]{:S(2)}) copy-start(bf16[2,8,3,128,128]{4,3,2,1,0:T(8,128)(2,1)} %lblk.1) | copy-start | bytes 4718596
  4.2 1.0 %copy-start.1 = (f32[256,384]{1,0:T(8,128)S(1)}, f32[256,384]{1,0:T(8,128)}, u32[]{:S(2)}) copy-start(f32[256,384]{1,0:T(8,128)} %meas_hbm.1) | copy-start | bytes 1179652
  5.2 1.0 %copy-start.2 = (f32[256,384]{1,0:T(8,128)S(1)}, f32[256,384]{1,0:T(8,128)}, u32[]{:S(2)}) copy-start(f32[256,384]{1,0:T(8,128)} %den_hbm.1) | copy-start | bytes 1179652

commit v4 on v3

--- a/solution.py
+++ b/solution.py
@@ -326,7 +326,7 @@
             dma((nrow - 1,)), dma((nrow - 1,)), dma((ncol - 1,)), dma((ncol - 1,)),
         ],
         compiler_params=pltpu.CompilerParams(
-            collective_id=0, has_side_effects=True, vmem_limit_bytes=48 * 1024 * 1024
+            collective_id=0, has_side_effects=True, vmem_limit_bytes=60 * 1024 * 1024
         ),
         name="conjugate",
     )(reg_weight, left_cols, right_cols, measured, denoised, left_blocks, right_blocks)

time: 77.2 us -> 76.3 us (0.988)
  Pallas kernels: 69.2 us -> 68.3 us
    pallas_call x1, Pallas kernels: 69.2 us -> 68.3 us  [shards(): pl.pallas_call(functools.partial(main_kernel, nrow, ncol, block), out_sha...]
    unnamed x10 -> x4, local copies, waits for them, and re-layouts: 6.43 us -> 6.27 us
where the time goes in v4:
time: 76.3 us; the launch traced here: 75.9 us
  Pallas kernels  68.3 us (90%)
  local copies, waits for them, and re-layouts  6.27 us (8%)
  between operations  1.29 us (2%)
    pallas_call x1, Pallas kernels, shards(): pl.pallas_call(functools.partial(main_kernel, nrow, ncol, block), out_sha...  68.3 us
    unnamed x4, local copies, waits for them, and re-layouts  6.27 us

profile of v4, /device:TPU:0, one launch (start us, length us, event | category | flops | bytes accessed | tf_op | source)
XLA Modules:
  0.0 75.9 jit_solution(14215578264103455023)
XLA Ops:
  1.3 1.4 %copy.9.lcols = s32[2,8,3]{2,1,0:T(8,128)} copy(s32[2,8,3]{1,0,2:T(2,128)} %param.11) | data formatting | bytes 384 | tf_op args[4]
  2.6 1.4 %copy.10.rcols = s32[2,24,3]{2,1,0:T(8,128)} copy(s32[2,24,3]{1,0,2:T(2,128)} %param.13) | data formatting | bytes 1152 | tf_op args[6]
  4.0 68.3 %conjugate.1 = (f32[256,384]{1,0:T(8,128)}, f32[256,384]{1,0:T(8,128)}) custom-call(f32[1]{0:T(128)S(6)} %copy.13.weight_ref, s32[2,8,3]{2,1,0:T(8,128)} %copy.9.lcols, s32[2,24,3]{2,1,0:T(8,128)} %copy.10.rcols, f32[256,384]{1,0:T(8,128)} %meas_hbm.1, f32[256,384]{1,0:T(8,128)} %den_hbm.1, bf16[2,8,3,128,128]{4,3,2,1,0:T(8,128)(2,1)} %lblk.1, ...), custom_call_target="tpu_custom_call" | custom-call | tf_op jit(solution)/shard_map/conjugate/pallas_call | solution.py:295
  72.4 1.8 %copy.14 = f32[256,384]{1,0:T(8,128)} copy(f32[256,384]{1,0:T(8,128)} %get-tuple-element.4) | data formatting | bytes 786432
  74.1 1.8 %copy.15 = f32[256,384]{1,0:T(8,128)} copy(f32[256,384]{1,0:T(8,128)} %get-tuple-element.5) | data formatting | bytes 786432

commit v5 on v4

--- a/solution.py
+++ b/solution.py
@@ -19,9 +19,9 @@
 
 def main_kernel(
     nrow, ncol, block,
-    weight_ref, lcols, rcols, meas_hbm, den_hbm, lblk, rblk,
+    weight_ref, lcols_hbm, rcols_hbm, meas_hbm, den_hbm, lblk, rblk,
     sol_ref, res_ref,
-    meas, den, lwin, rwin, bf_ref, ba_ref, af_ref, aa_ref,
+    lcols, rcols, meas, den, lwin, rwin, bf_ref, ba_ref, af_ref, aa_ref,
     xo, xl, xr, wo, pu, pd, ru, rd, v0, v1, v2, stat, rstat, cstat,
     msem, lsem, rsem, xsend, xrecv, wsend, wrecv, rsend, rrecv, csend, crecv,
 ):
@@ -40,6 +40,10 @@
     load_meas = pltpu.make_async_copy(meas_hbm, meas, msem.at[0])
     load_den = pltpu.make_async_copy(den_hbm, den, msem.at[1])
     load_meas.start()
+    load_lcols = pltpu.make_async_copy(lcols_hbm, lcols, msem.at[2])
+    load_rcols = pltpu.make_async_copy(rcols_hbm, rcols, msem.at[3])
+    load_lcols.start()
+    load_rcols.start()
 
     def fetch(source, window, sem, first, total, count):
         return [
@@ -111,6 +115,7 @@
     empty = jnp.zeros((block, block), BF16)
 
     def build_ba():
+        load_rcols.wait()
         for copy in load_right:
             copy.wait()
         for k in range(2):
@@ -139,6 +144,7 @@
                         bf_ref[k, span(t), span(c)] = empty
 
     def build_aa():
+        load_lcols.wait()
         for copy in load_left:
             copy.wait()
         for k in range(2):
@@ -192,12 +198,13 @@
         acc = [dot(xo[index], bmat[k, pl.ds(halo, width), :]) for k in range(2)]
         for q in chunks:
             to_right, to_left = sides[q]
+            near = [acc[k][q * block : (q + 1) * block] for k in range(2)]
             pl.when(has_left)(to_right.wait_recv)
+            for k in range(2):
+                near[k] = near[k] + dot(xl[index, span(q)], bmat[k, pl.ds(0, halo), :])
             pl.when(has_right)(to_left.wait_recv)
             for k in range(2):
-                total = acc[k][q * block : (q + 1) * block]
-                total = total + dot(xl[index, span(q)], bmat[k, pl.ds(0, halo), :])
-                total = total + dot(xr[index, span(q)], bmat[k, pl.ds(halo + width, halo), :])
+                total = near[k] + dot(xr[index, span(q)], bmat[k, pl.ds(halo + width, halo), :])
                 wo[span(k * own_rows + q)] = total.astype(BF16)
         if fill_a is not None:
             fill_a()
@@ -218,6 +225,21 @@
         pl.when(has_up)(to_down.wait_recv)
         pl.when(has_down)(to_up.wait_recv)
         return out + ru[index].astype(F32) + rd[index].astype(F32)
+
+    def lanes(a, b):
+        folded = jnp.sum(a[...] * b[...], axis=0, keepdims=True)
+        total = folded[:, 0:128]
+        for start in range(128, width, 128):
+            total = total + folded[:, start : start + 128]
+        return total
+
+    def products_from(pairs, first_slot):
+        for slot, (a, b) in enumerate(pairs):
+            stat[0, pl.ds(first_slot + slot, 1), :] = lanes(a, b)
+
+    def early():
+        products_from(((v0, v0), (v0, v1), (v1, v1)), 0)
+        stat[0, pl.ds(5, 3), :] = jnp.zeros((3, 128), F32)
 
     weight = weight_ref[0]
     first = operate(0, ba_ref, aa_ref, build_ba, build_aa)
@@ -230,18 +252,9 @@
     xo[3] = second.astype(BF16)
     v1[...] = second
     xo[4] = operate(3, bf_ref, af_ref).astype(BF16)
-    v2[...] = operate(4, ba_ref, aa_ref) + weight * v1[...]
-
-    def lanes(a, b):
-        folded = jnp.sum(a[...] * b[...], axis=0, keepdims=True)
-        total = folded[:, 0:128]
-        for start in range(128, width, 128):
-            total = total + folded[:, start : start + 128]
-        return total
-
-    for slot, (a, b) in enumerate(((v0, v0), (v0, v1), (v1, v1), (v0, v2), (v1, v2))):
-        stat[0, pl.ds(slot, 1), :] = lanes(a, b)
-    stat[0, pl.ds(5, 3), :] = jnp.zeros((3, 128), F32)
+    v2[...] = operate(4, ba_ref, aa_ref, early) + weight * v1[...]
+
+    products_from(((v0, v2), (v1, v2)), 3)
 
     def gather(source, slots, send, recv, count, device):
         copies = [
@@ -295,9 +308,11 @@
     return pl.pallas_call(
         functools.partial(main_kernel, nrow, ncol, block),
         out_shape=[jax.ShapeDtypeStruct((height, width), F32)] * 2,
-        in_specs=[smem] * 3 + [hbm] * 4,
+        in_specs=[smem] + [hbm] * 6,
         out_specs=[pl.BlockSpec(memory_space=pltpu.VMEM)] * 2,
         scratch_shapes=[
+            pltpu.SMEM(left_cols.shape, jnp.int32),
+            pltpu.SMEM(right_cols.shape, jnp.int32),
             field,
             field,
             pltpu.VMEM((2, own_rows + 4, 3, block, block), BF16),
@@ -320,7 +335,7 @@
             pltpu.VMEM((2, 8, 128), F32),
             pltpu.VMEM((nrow - 1, 8, 128), F32),
             pltpu.VMEM((ncol - 1, 8, 128), F32),
-            dma((2,)), dma((2, own_rows + 4)), dma((2, own_cols + 4)),
+            dma((4,)), dma((2, own_rows + 4)), dma((2, own_cols + 4)),
             dma((OPS, own_rows, 2)), dma((OPS, own_rows, 2)),
             dma((OPS, 2)), dma((OPS, 2)),
             dma((nrow - 1,)), dma((nrow - 1,)), dma((ncol - 1,)), dma((ncol - 1,)),

time: 76.3 us -> 75.2 us (0.986)
  Pallas kernels: 68.3 us -> 67.4 us
    pallas_call x1, Pallas kernels: 68.3 us -> 67.4 us  [shards(): pl.pallas_call(functools.partial(main_kernel, nrow, ncol, block), out_sha...]
where the time goes in v5:
time: 75.2 us; the launch traced here: 74.9 us
  Pallas kernels  67.4 us (90%)
  local copies, waits for them, and re-layouts  6.27 us (8%)
  between operations  1.29 us (2%)
    pallas_call x1, Pallas kernels, shards(): pl.pallas_call(functools.partial(main_kernel, nrow, ncol, block), out_sha...  67.4 us
    unnamed x4, local copies, waits for them, and re-layouts  6.27 us

profile of v5, /device:TPU:0, one launch (start us, length us, event | category | flops | bytes accessed | tf_op | source)
XLA Modules:
  0.0 74.9 jit_solution(958659771205462713)
XLA Ops:
  1.3 1.4 %copy.9.lcols_hbm = s32[2,8,3]{2,1,0:T(8,128)} copy(s32[2,8,3]{1,0,2:T(2,128)} %param.11) | data formatting | bytes 384 | tf_op args[4]
  2.6 1.4 %copy.10.rcols_hbm = s32[2,24,3]{2,1,0:T(8,128)} copy(s32[2,24,3]{1,0,2:T(2,128)} %param.13) | data formatting | bytes 1152 | tf_op args[6]
  4.0 67.4 %conjugate.1 = (f32[256,384]{1,0:T(8,128)}, f32[256,384]{1,0:T(8,128)}) custom-call(f32[1]{0:T(128)S(6)} %copy.13.weight_ref, s32[2,8,3]{2,1,0:T(8,128)} %copy.9.lcols_hbm, s32[2,24,3]{2,1,0:T(8,128)} %copy.10.rcols_hbm, f32[256,384]{1,0:T(8,128)} %meas_hbm.1, f32[256,384]{1,0:T(8,128)} %den_hbm.1, bf16[2,8,3,128,128]{4,3,2,1,0:T(8,128)(2,1)} %lblk.1, ...), custom_call_target="tpu_custom_call" | custom-call | tf_op jit(solution)/shard_map/conjugate/pallas_call | solution.py:308
  71.4 1.8 %copy.14 = f32[256,384]{1,0:T(8,128)} copy(f32[256,384]{1,0:T(8,128)} %get-tuple-element.4) | data formatting | bytes 786432
  73.2 1.8 %copy.15 = f32[256,384]{1,0:T(8,128)} copy(f32[256,384]{1,0:T(8,128)} %get-tuple-element.5) | data formatting | bytes 786432
